TPU v7x, 128 devices: a whole 4x4x4 slice. The times are simulated.
128 devices in a mesh: group: 4 (over x), bulk: 32 (over z, y, core).
Axes of the slice: x: 4, y: 4, z: 4, core: 2. Of those that a mesh axis runs over, the one named last changes fastest.
Arguments:
- rhs: float32 [512, 64, 128], P(('group', 'bulk')), may hold values from -90 to 90, as said below
- diag_tiles: float32 [512, 128, 128], P(('group', 'bulk')), may hold values from -0.06 to 0.06
- offdiag_blocks: float32 [512, 11, 128, 128], P(('group', 'bulk')), may hold values from -0.026 to 0.026
- coupling: float32 [256, 4, 128, 128], P(('group', 'bulk')), may hold values from -0.05 to 0.05, as said below
- col_index: int32 [512, 11], replicated, may hold values from 0 to 511, as said below
- load: int32 [512], replicated, may hold values from 3 to 11
- new_slot: int32 [512], replicated, may hold values from 0 to 511, as said below
Outputs:
- solution_out: float32 [512, 64, 128], P(('group', 'bulk'))
- residual_out: float32 [512, 64, 128], P(('group', 'bulk'))
Inputs may be any that keep to these rules, and one draw needn't show every extreme that they name: `rhs`: made of random entries times scales of the rows and of the columns. `coupling`: entry [d * 2 + k, h] is the transpose of entry [(h * 32 + d % 32) * 2 + k, d // 32]. `col_index`: for each part g and each tile position t, the column t of the 128 block rows of part g is a permutation of that part's slots g * 128 to (g + 1) * 128 - 1. Of the 44 entries of the 4 block rows of one device (slots d * 4 to (d + 1) * 4 - 1), at most 2 name slots of any one device, and exactly 2 name slots of some device. `new_slot`: A permutation. On every device exactly one block row moves, from a slot k with 2 <= k % 4; it stays in its part, goes from owner b to owner b XOR m, where m (1 to 31) is one number for the whole part, and takes the slot that the moving row of that device leaves.
All inputs are finite; a program needn't handle non-finite values.
Results may differ from a plain program's by a relative error of at most 0.0003.
Values sent between devices are 32-bit elements; how exact they have to be, the bound alone decides.
A program may use at most 64 MiB of HBM per device.

v0:
```python
import jax
import jax.numpy as jnp
from jax import lax
from jax.sharding import PartitionSpec as P

highest = lax.Precision.HIGHEST
diagonal_shift = 4.0


def from_partner(value, axis, bit):
    mask = 2**bit
    pairs = [(source, source ^ mask) for source in range(lax.axis_size(axis))]
    return lax.ppermute(value, axis, pairs)


def chol_apply(matrix, right):
    factor = jnp.linalg.cholesky(matrix)
    middle = lax.linalg.triangular_solve(factor, right, left_side=True, lower=True)
    return lax.linalg.triangular_solve(factor, middle, left_side=True, lower=True, transpose_a=True)


def global_gram(left, right):
    partial_gram = jnp.einsum("snt,smt->nm", left, right, precision=highest)
    total = lax.psum(partial_gram, ("group", "bulk"))
    return 0.5 * (total + total.T)


def operate(vectors, diag, masked, column_ids, coupling):
    row_count = vectors.shape[0]
    boundary_rows = coupling.shape[0]
    part_count = coupling.shape[1]
    group_rows = row_count * lax.axis_size("bulk")
    border = lax.all_gather(vectors[:boundary_rows], "group", axis=0, tiled=True)
    final_output = diagonal_shift * vectors + jnp.einsum(
        "rnj,rij->rni", vectors, diag, precision=highest
    )
    returned = jnp.einsum("rni,rkij->rknj", vectors, masked, precision=highest)
    flat_terms = returned.reshape((-1,) + vectors.shape[1:])
    panel = lax.all_gather(vectors, "bulk", axis=0, tiled=True)
    buffer = jax.ops.segment_sum(flat_terms, column_ids.reshape(-1), num_segments=group_rows)
    owed = lax.psum_scatter(buffer, "bulk", scatter_dimension=0, tiled=True)
    picked = panel[column_ids]
    final_output = (
        final_output + jnp.einsum("rknj,rkij->rni", picked, masked, precision=highest) + owed
    )
    border = border.reshape((part_count, boundary_rows) + vectors.shape[1:])
    crossed = jnp.einsum("khij,hknj->kni", coupling, border, precision=highest)
    return final_output.at[:boundary_rows].add(crossed)


def advance(state, diag, masked, column_ids, coupling, last_step):
    solution, resid, direction, gram_rr = state
    image = operate(direction, diag, masked, column_ids, coupling)
    gram_pq = global_gram(direction, image)
    alpha = chol_apply(gram_pq, gram_rr)
    solution = solution + jnp.einsum("mn,smt->snt", alpha, direction, precision=highest)
    resid = resid - jnp.einsum("mn,smt->snt", alpha, image, precision=highest)
    if not last_step:
        gram_new = global_gram(resid, resid)
        beta = chol_apply(gram_rr, gram_new)
        direction = resid + jnp.einsum("mn,smt->snt", beta, direction, precision=highest)
        gram_rr = gram_new
    return (solution, resid, direction, gram_rr)


def local(rhs, diag_tiles, offdiag_blocks, coupling, col_index, load, new_slot):
    row_count = rhs.shape[0]
    off_count = offdiag_blocks.shape[1]
    bulk_count = lax.axis_size("bulk")
    group_rows = row_count * bulk_count
    my_group = lax.axis_index("group")
    my_bulk = lax.axis_index("bulk")
    first_slot = (my_group * bulk_count + my_bulk) * row_count
    group_base = my_group * group_rows
    own_slots = first_slot + jnp.arange(row_count, dtype=jnp.int32)
    tile_ids = jnp.arange(off_count, dtype=jnp.int32)
    old_columns = col_index[own_slots] - group_base
    old_mask = (tile_ids[None, :] < load[own_slots][:, None]).astype(jnp.float32)
    old_masked = offdiag_blocks * old_mask[:, :, None, None]
    own_new = new_slot[own_slots]
    leaving = jnp.argmax((own_new != own_slots).astype(jnp.int32))
    target = own_new[leaving]
    target_bulk = target // row_count % bulk_count
    xor_mask = jnp.bitwise_xor(target_bulk, my_bulk)
    start_state = (jnp.zeros_like(rhs), rhs, rhs, global_gram(rhs, rhs))
    state = advance(start_state, diag_tiles, old_masked, old_columns, coupling, False)
    solution, resid, direction, gram_rr = state
    pieces = [
        offdiag_blocks[leaving],
        diag_tiles[leaving],
        solution[leaving],
        resid[leaving],
        direction[leaving],
    ]
    flat = jnp.concatenate([piece.reshape(-1) for piece in pieces])
    for bit_pos in range(bulk_count.bit_length() - 1):
        partner = from_partner(flat, "bulk", bit_pos)
        chosen = jnp.bitwise_and(jnp.right_shift(xor_mask, bit_pos), 1) == 1
        flat = jnp.where(chosen, partner, flat)
    outputs = []
    offset = 0
    for piece in pieces:
        outputs.append(flat[offset : offset + piece.size].reshape(piece.shape))
        offset = offset + piece.size
    moved_off = offdiag_blocks.at[leaving].set(outputs[0])
    moved_diag = diag_tiles.at[leaving].set(outputs[1])
    solution = solution.at[leaving].set(outputs[2])
    resid = resid.at[leaving].set(outputs[3])
    direction = direction.at[leaving].set(outputs[4])
    inverse = (
        jnp.zeros_like(new_slot).at[new_slot].set(jnp.arange(new_slot.shape[0], dtype=jnp.int32))
    )
    old_rows = inverse[own_slots]
    new_columns = new_slot[col_index[old_rows]] - group_base
    new_mask = (tile_ids[None, :] < load[old_rows][:, None]).astype(jnp.float32)
    new_masked = moved_off * new_mask[:, :, None, None]
    state = advance(
        (solution, resid, direction, gram_rr), moved_diag, new_masked, new_columns, coupling, True
    )
    return (state[0], state[1])


def solution(mesh):
    return jax.shard_map(
        local,
        mesh=mesh,
        in_specs=(
            P(("group", "bulk"), None, None),
            P(("group", "bulk"), None, None),
            P(("group", "bulk"), None, None, None),
            P(("group", "bulk"), None, None, None),
            P(),
            P(),
            P(),
        ),
        out_specs=(P(("group", "bulk"), None, None), P(("group", "bulk"), None, None)),
        check_vma=False,
    )
```

profile of v0, /device:TPU:1, one launch (start us, length us, event | category | flops | bytes accessed | tf_op | source)
XLA Modules:
  0.0 662.4 jit_solution(1041182074401895514)
XLA Ops:
  31.0 8.0 %scatter_fusion = f32[128,64,128]{2,1,0:T(8,128)} fusion(f32[128,64,128]{2,1,0:T(8,128)} %broadcast.320.clone, s32[44]{0:T(128)} %reshape.516, f32[44,64,128]{2,1,0:T(8,128)} %bitcast.222), kind=kCustom, calls=%fused_computation.9 | custom fusion | flops 360448 | bytes 4325552 | tf_op jit(solution)/shard_map/scatter-add | solution.py:40
  45.5 13.0 %all_gather.13 = f32[8,64,128]{2,1,0:T(8,128)} all-gather(f32[2,64,128]{2,1,0:T(8,128)} %slice.208), channel_id=1, replica_groups=mesh['group'=4,'bulk'=32] {'group'}, dimensions={0}, use_global_device_ids=true | all-gather | bytes 327680 | tf_op jit(solution)/shard_map/all_gather | solution.py:33
  62.4 4.0 gather_fusion.1
  66.4 5.4 fusion.12
  71.8 71.6 %reduce-scatter.3.cloned.1.call-done = f32[4,64,128]{2,1,0:T(8,128)} async-done(((f32[128,64,128]{2,1,0:T(8,128)}), f32[4,64,128]{2,1,0:T(8,128)}) %reduce-scatter.3.cloned.1.call-update) | async-done | bytes 131088 | tf_op jit(solution)/shard_map/reduce_scatter | solution.py:41
  148.2 66.3 %all-reduce = (f32[64,64]{1,0:T(8,128)}, f32[64,64]{1,0:T(8,128)}) all-reduce(f32[64,64]{1,0:T(8,128)} %convolution_bitcast_fusion.11, f32[64,64]{1,0:T(8,128)} %convolution_bitcast_fusion.12), channel_id=1, replica_groups=mesh['group'=4,'bulk'=32] {'group','bulk'}, use_global_device_ids=true, to_apply=%region_5.7 | all-reduce | flops 8192 | bytes 65536 | tf_op jit(solution)/shard_map/psum | solution.py:24
  224.5 7.2 %cholesky.59 = f32[64,64]{1,0:T(8,128)} custom-call(f32[64,64]{1,0:T(8,128)} %fusion.60), custom_call_target="Cholesky" | custom-call | tf_op jit(solution)/shard_map/jit(cholesky)/cholesky | solution.py:17
  235.3 6.3 custom-call.13
  247.7 7.2 %cholesky.70 = f32[64,64]{1,0:T(8,128)} custom-call(f32[64,64]{1,0:T(8,128)} %fusion.55), custom_call_target="Cholesky" | custom-call | tf_op jit(solution)/shard_map/jit(cholesky)/cholesky | solution.py:17
  258.5 6.3 custom-call.15
  266.6 63.0 %psum.30 = f32[64,64]{1,0:T(8,128)} all-reduce(f32[64,64]{1,0:T(8,128)} %convolution_bitcast_fusion.9), channel_id=1, replica_groups=mesh['group'=4,'bulk'=32] {'group','bulk'}, use_global_device_ids=true, to_apply=%region_8.12 | all-reduce | flops 4096 | bytes 32768 | tf_op jit(solution)/shard_map/psum | solution.py:24
  344.7 20.3 %collective-permute-done.1 = f32[221184]{0:T(1024)} collective-permute-done((f32[221184]{0:T(1024)}, f32[221184]{0:T(1024)}, u32[]{:S(2)}, u32[]{:S(2)}) %collective-permute-start.1) | collective-permute-done | bytes 884768 | tf_op jit(solution)/shard_map/ppermute | solution.py:13
  370.2 19.2 %collective-permute-done.2 = f32[221184]{0:T(1024)} collective-permute-done((f32[221184]{0:T(1024)}, f32[221184]{0:T(1024)}, u32[]{:S(2)}, u32[]{:S(2)}) %collective-permute-start.2) | collective-permute-done | bytes 884768 | tf_op jit(solution)/shard_map/ppermute | solution.py:13
  392.7 18.7 %collective-permute-done.3 = f32[221184]{0:T(1024)} collective-permute-done((f32[221184]{0:T(1024)}, f32[221184]{0:T(1024)}, u32[]{:S(2)}, u32[]{:S(2)}) %collective-permute-start.3) | collective-permute-done | bytes 884768 | tf_op jit(solution)/shard_map/ppermute | solution.py:13
  416.7 17.4 %collective-permute-done.4 = f32[221184]{0:T(1024)} collective-permute-done((f32[221184]{0:T(1024)}, f32[221184]{0:T(1024)}, u32[]{:S(2)}, u32[]{:S(2)}) %collective-permute-start.4) | collective-permute-done | bytes 884768 | tf_op jit(solution)/shard_map/ppermute | solution.py:13
  451.1 7.8 %scatter_fusion.1 = f32[128,64,128]{2,1,0:T(8,128)} fusion(f32[128,64,128]{2,1,0:T(8,128)} %broadcast.320, s32[44]{0:T(128)S(1)} %broadcast_subtract_fusion.1, f32[44,64,128]{2,1,0:T(8,128)} %bitcast.223), kind=kCustom, calls=%fused_computation.11 | custom fusion | flops 360448 | bytes 4325552 | tf_op jit(solution)/shard_map/scatter-add | solution.py:40
  459.2 10.1 %all_gather.15 = f32[8,64,128]{2,1,0:T(8,128)} all-gather(f32[2,64,128]{2,1,0:T(8,128)S(1)} %slice.243), channel_id=1, replica_groups=mesh['group'=4,'bulk'=32] {'group'}, dimensions={0}, use_global_device_ids=true | all-gather | bytes 327680 | tf_op jit(solution)/shard_map/all_gather | solution.py:33
  471.4 15.3 %all-gather.5.cloned.1.call-done = f32[128,64,128]{2,1,0:T(8,128)} async-done(((f32[4,64,128]{2,1,0:T(8,128)}), f32[128,64,128]{2,1,0:T(8,128)}) %all-gather.5.cloned.1.call-update) | async-done | bytes 4194320 | tf_op jit(solution)/shard_map/all_gather | solution.py:39
  486.7 4.0 gather_fusion.7
  490.7 5.4 fusion.15
  496.2 73.8 %reduce-scatter.5.cloned.1.call-done = f32[4,64,128]{2,1,0:T(8,128)} async-done(((f32[128,64,128]{2,1,0:T(8,128)}), f32[4,64,128]{2,1,0:T(8,128)}) %reduce-scatter.5.cloned.1.call-update) | async-done | bytes 131088 | tf_op jit(solution)/shard_map/reduce_scatter | solution.py:41
  573.5 66.0 %psum.31 = f32[64,64]{1,0:T(8,128)S(1)} all-reduce(f32[64,64]{1,0:T(8,128)S(1)} %convolution_bitcast_fusion.7), channel_id=1, replica_groups=mesh['group'=4,'bulk'=32] {'group','bulk'}, use_global_device_ids=true, to_apply=%region_13.17 | all-reduce | flops 4096 | bytes 32768 | tf_op jit(solution)/shard_map/psum | solution.py:24
  639.7 5.8 cholesky.81
  646.9 4.9 custom-call.17
  (142 shorter events, 116.7 us)
Async XLA Ops:
  7.2 137.9 %copy-start = (f32[2,4,128,128]{3,2,1,0:T(8,128)S(1)}, f32[2,4,128,128]{3,2,1,0:T(8,128)}, u32[]{:S(2)}) copy-start(f32[2,4,128,128]{3,2,1,0:T(8,128)} %param.29) | copy-start | bytes 1572868
  7.2 18.1 %copy-start.3 = (f32[4,64,128]{2,1,0:T(8,128)S(1)}, f32[4,64,128]{2,1,0:T(8,128)}, u32[]{:S(2)}) copy-start(f32[4,64,128]{2,1,0:T(8,128)} %param.26) | copy-start | bytes 393220
  7.2 16.2 %copy-start.2 = (s32[512]{0:T(512)S(1)}, s32[512]{0:T(512)}, u32[]{:S(2)}) copy-start(s32[512]{0:T(512)} %param.31) | copy-start | bytes 6148
  7.2 4.3 copy-start.1
  7.2 55.2 %all-gather.3.cloned.1.call-start = ((), (), s32[]{:S(2)}) async-start(), calls=%async_computation.2 | async-start | bytes 4325376 | tf_op jit(solution)/shard_map/all_gather | solution.py:39
  7.3 1.9 copy-start.11
  9.9 133.5 %reduce-scatter.3.cloned.1.call-start = ((), (), s32[]{:S(2)}) async-start(), calls=%async_computation.3 | async-start | bytes 4325376 | tf_op jit(solution)/shard_map/reduce_scatter | solution.py:41
  39.0 447.7 %all-gather.5.cloned.1.call-start = ((), (), s32[]{:S(2)}) async-start(), calls=%async_computation.4 | async-start | bytes 4325376 | tf_op jit(solution)/shard_map/all_gather | solution.py:39
  71.8 266.4 %copy-start.13 = (s32[4]{0:T(128)S(1)}, s32[4]{0:T(128)}, u32[]{:S(2)}) copy-start(s32[4]{0:T(128)} %gather_fusion.3) | copy-start | bytes 52
  146.7 0.7 copy-start.7
  334.2 2.8 copy-start.4
  337.6 3.7 collective-permute-start
  343.5 21.5 %collective-permute-start.1 = (f32[221184]{0:T(1024)}, f32[221184]{0:T(1024)}, u32[]{:S(2)}, u32[]{:S(2)}) collective-permute-start(f32[221184]{0:T(1024)} %broadcast_select_fusion), channel_id=1, source_target_pairs={{0,2},{1,3},{2,0},{3,1},{4,6},{5,7},{6,4},{7,5},{8,10},{9,11},{10,... | collective-permute-start | bytes 2654216 | tf_op jit(solution)/shard_map/ppermute | solution.py:13
  367.2 48.7 %copy-start.14 = (s32[3]{0:T(128)S(1)}, s32[3]{0:T(128)}, u32[]{:S(2)}) copy-start(s32[3]{0:T(128)} %constant.237.clone.1) | copy-start | bytes 40
  367.2 49.5 %copy-start.8 = (f32[64,4,128]{2,0,1:T(8,128)S(1)}, f32[64,4,128]{2,0,1:T(8,128)}, u32[]{:S(2)}) copy-start(f32[64,4,128]{2,0,1:T(8,128)} %fusion.73) | copy-start | bytes 393220
  367.2 22.2 %collective-permute-start.2 = (f32[221184]{0:T(1024)}, f32[221184]{0:T(1024)}, u32[]{:S(2)}, u32[]{:S(2)}) collective-permute-start(f32[221184]{0:T(1024)} %broadcast_select_fusion.1), channel_id=1, source_target_pairs={{0,4},{1,5},{2,6},{3,7},{4,0},{5,1},{6,2},{7,3},{8,12},{9,13},{10,... | collective-permute-start | bytes 2654216 | tf_op jit(solution)/shard_map/ppermute | solution.py:13
  391.6 19.8 %collective-permute-start.3 = (f32[221184]{0:T(1024)}, f32[221184]{0:T(1024)}, u32[]{:S(2)}, u32[]{:S(2)}) collective-permute-start(f32[221184]{0:T(1024)} %broadcast_select_fusion.2), channel_id=1, source_target_pairs={{0,8},{1,9},{2,10},{3,11},{4,12},{5,13},{6,14},{7,15},{8,0},{9,1},... | collective-permute-start | bytes 2654216 | tf_op jit(solution)/shard_map/ppermute | solution.py:13
  392.7 47.8 %copy-start.12 = (s32[4,11,1]{1,0,2:T(4,128)S(1)}, s32[4,11,1]{1,0,2:T(4,128)}, u32[]{:S(2)}) copy-start(s32[4,11,1]{1,0,2:T(4,128)} %get-tuple-element.98) | copy-start | bytes 532
  413.6 20.5 %collective-permute-start.4 = (f32[221184]{0:T(1024)}, f32[221184]{0:T(1024)}, u32[]{:S(2)}, u32[]{:S(2)}) collective-permute-start(f32[221184]{0:T(1024)} %broadcast_select_fusion.3), channel_id=1, source_target_pairs={{0,16},{1,17},{2,18},{3,19},{4,20},{5,21},{6,22},{7,23},{8,24},{9,... | collective-permute-start | bytes 2654216 | tf_op jit(solution)/shard_map/ppermute | solution.py:13
  435.3 0.9 copy-start.6
  438.3 0.7 copy-start.9
  438.9 131.0 %reduce-scatter.5.cloned.1.call-start = ((), (), s32[]{:S(2)}) async-start(), calls=%async_computation.5 | async-start | bytes 4325376 | tf_op jit(solution)/shard_map/reduce_scatter | solution.py:41
  440.5 4.9 copy-start.5
  496.2 158.8 %copy-start.10 = (f32[4,64,128]{2,1,0:T(8,128)S(1)}, f32[4,64,128]{2,1,0:T(8,128)}, u32[]{:S(2)}) copy-start(f32[4,64,128]{2,1,0:T(8,128)} %copy-done.9) | copy-start | bytes 393220
Sparse Core Ops, SparseCore 0:
  10.3 49.7 all-gather.2
  63.7 79.6 reduce-scatter.2
  439.1 47.6 all-gather.4
  490.2 79.7 reduce-scatter.4
where the time goes:
time: 666 us; the launch traced here: 662 us
  waiting for transfers between devices  236 us (35%)
  blocking collectives  218 us (33%)
  other arithmetic  90.6 us (14%)
  local copies, waits for them, and re-layouts  50.3 us (8%)
  matrix products  39.5 us (6%)
  between operations  18.6 us (3%)
  starting transfers between devices  8.54 us (1%)
    psum x3, blocking collectives, global_gram(): total = lax.psum(partial_gram, ('group', 'bulk'))  195 us
    reduce_scatter x2, waiting for transfers between devices, operate(): owed = lax.psum_scatter(buffer, 'bulk', scatter_dimension=0, tiled=True)  145 us
    ppermute x5, waiting for transfers between devices, from_partner(): return lax.ppermute(value, axis, pairs)  75.6 us
    another operation x9, other arithmetic, chol_apply(): factor = jnp.linalg.cholesky(matrix)  23.9 us
    all_gather x2, blocking collectives, operate(): lax.all_gather(vectors[:boundary_rows], 'group', axis=0, tiled=True)  23.1 us
    another operation x6, other arithmetic, chol_apply(): lax.linalg.triangular_solve(factor, middle, left_side=True, lower=True, t...  22.2 us
    scatter-add x2, other arithmetic, operate(): jax.ops.segment_sum(flat_terms, column_ids.reshape(-1), num_segments=grou...  15.8 us
    all_gather x2, waiting for transfers between devices, operate(): panel = lax.all_gather(vectors, 'bulk', axis=0, tiled=True)  15.3 us
  transfers between devices with their start and end apart: 9, of which 7 were waited for; matrix products, arithmetic and copies ran while one was open for 12% of the time, Pallas kernels for 0%

commit v1 on v0

--- a/solution.py
+++ b/solution.py
@@ -21,7 +21,8 @@
 
 def global_gram(left, right):
     partial_gram = jnp.einsum("snt,smt->nm", left, right, precision=highest)
-    total = lax.psum(partial_gram, ("group", "bulk"))
+    s_next = lax.all_gather(partial_gram, axis_name=("group", "bulk"))
+    total = jnp.sum(s_next, axis=0)
     return 0.5 * (total + total.T)
 
 

time: 666 us -> 717 us (1.077)
  waiting for transfers between devices: 236 us -> 477 us
  blocking collectives: 218 us -> 23.3 us
  other arithmetic: 90.6 us -> 102 us
    all_gather x0 -> x4, waiting for transfers between devices: none -> 229 us  [global_gram(): s_next = lax.all_gather(partial_gram, axis_name=('group', 'bulk'))]
    psum x3 -> x0, blocking collectives: 195 us -> none  [global_gram(): total = lax.psum(partial_gram, ('group', 'bulk'))]
    reduce_sum x0 -> x4, other arithmetic: none -> 11.9 us  [global_gram(): total = jnp.sum(s_next, axis=0)]
    unnamed x38 -> x53, local copies, waits for them, and re-layouts: 11.6 us -> 14.8 us
  transfers between devices with their start and end apart: 9 -> 13, of which waited for: 7 -> 12; matrix products, arithmetic and copies ran while one was open for 12% -> 16% of each run, Pallas kernels for 0% -> 0%
where the time goes in v1:
time: 717 us; the launch traced here: 714 us
  waiting for transfers between devices  477 us (67%)
  other arithmetic  102 us (14%)
  local copies, waits for them, and re-layouts  52.3 us (7%)
  matrix products  36.8 us (5%)
  blocking collectives  23.3 us (3%)
  between operations  19 us (3%)
    all_gather x4, waiting for transfers between devices, global_gram(): s_next = lax.all_gather(partial_gram, axis_name=('group', 'bulk'))  229 us
    reduce_scatter x2, waiting for transfers between devices, operate(): owed = lax.psum_scatter(buffer, 'bulk', scatter_dimension=0, tiled=True)  148 us
    ppermute x5, waiting for transfers between devices, from_partner(): return lax.ppermute(value, axis, pairs)  80 us
    another operation x9, other arithmetic, chol_apply(): factor = jnp.linalg.cholesky(matrix)  23.9 us
    all_gather x2, blocking collectives, operate(): lax.all_gather(vectors[:boundary_rows], 'group', axis=0, tiled=True)  23.3 us
    another operation x6, other arithmetic, chol_apply(): lax.linalg.triangular_solve(factor, middle, left_side=True, lower=True, t...  22.2 us
    all_gather x2, waiting for transfers between devices, operate(): panel = lax.all_gather(vectors, 'bulk', axis=0, tiled=True)  19.9 us
    scatter-add x2, other arithmetic, operate(): jax.ops.segment_sum(flat_terms, column_ids.reshape(-1), num_segments=grou...  15.8 us
  transfers between devices with their start and end apart: 13, of which 12 were waited for; matrix products, arithmetic and copies ran while one was open for 16% of the time, Pallas kernels for 0%

profile of v1, /device:TPU:1, one launch (start us, length us, event | category | flops | bytes accessed | tf_op | source)
XLA Modules:
  0.0 714.1 jit_solution(12491313526976643210)
XLA Ops:
  30.9 8.0 %scatter_fusion = f32[128,64,128]{2,1,0:T(8,128)} fusion(f32[128,64,128]{2,1,0:T(8,128)} %broadcast.320.clone, s32[44]{0:T(128)} %reshape.516, f32[44,64,128]{2,1,0:T(8,128)} %bitcast.226), kind=kCustom, calls=%fused_computation.9 | custom fusion | flops 360448 | bytes 4325552 | tf_op jit(solution)/shard_map/scatter-add | solution.py:41
  41.1 13.2 %all_gather.37 = f32[8,64,128]{2,1,0:T(8,128)} all-gather(f32[2,64,128]{2,1,0:T(8,128)} %slice.208), channel_id=1, replica_groups=mesh['group'=4,'bulk'=32] {'group'}, dimensions={0}, use_global_device_ids=true | all-gather | bytes 327680 | tf_op jit(solution)/shard_map/all_gather | solution.py:34
  55.0 5.1 all-gather.11.cloned.1.call-done
  64.1 5.4 fusion.12
  69.5 73.9 %reduce-scatter.3.cloned.1.call-done = f32[4,64,128]{2,1,0:T(8,128)} async-done(((f32[128,64,128]{2,1,0:T(8,128)}), f32[4,64,128]{2,1,0:T(8,128)}) %reduce-scatter.3.cloned.1.call-update) | async-done | bytes 131088 | tf_op jit(solution)/shard_map/reduce_scatter | solution.py:42
  150.7 64.4 %all-gather.17.cloned.1.call-done = f32[8192,64]{1,0:T(8,128)} async-done(((f32[64,64]{1,0:T(8,128)}), f32[8192,64]{1,0:T(8,128)}) %all-gather.17.cloned.1.call-update) | async-done | bytes 2097168 | tf_op jit(solution)/shard_map/all_gather | solution.py:24
  221.0 61.3 %all-gather.15.cloned.1.call-done = f32[8192,64]{1,0:T(8,128)} async-done(((f32[64,64]{1,0:T(8,128)}), f32[8192,64]{1,0:T(8,128)}) %all-gather.15.cloned.1.call-update) | async-done | bytes 2097168 | tf_op jit(solution)/shard_map/all_gather | solution.py:24
  291.1 7.2 %cholesky.59 = f32[64,64]{1,0:T(8,128)} custom-call(f32[64,64]{1,0:T(8,128)} %fusion.60), custom_call_target="Cholesky" | custom-call | tf_op jit(solution)/shard_map/jit(cholesky)/cholesky | solution.py:17
  301.8 6.3 custom-call.13
  321.4 7.2 %cholesky.70 = f32[64,64]{1,0:T(8,128)} custom-call(f32[64,64]{1,0:T(8,128)} %fusion.55), custom_call_target="Cholesky" | custom-call | tf_op jit(solution)/shard_map/jit(cholesky)/cholesky | solution.py:17
  332.2 6.3 custom-call.15
  342.1 35.8 %all-gather.19.cloned.1.call-done = f32[8192,64]{1,0:T(8,128)} async-done(((f32[64,64]{1,0:T(8,128)}), f32[8192,64]{1,0:T(8,128)}) %all-gather.19.cloned.1.call-update) | async-done | bytes 2097168 | tf_op jit(solution)/shard_map/all_gather | solution.py:24
  392.6 21.3 %collective-permute-done.1 = f32[221184]{0:T(1024)} collective-permute-done((f32[221184]{0:T(1024)}, f32[221184]{0:T(1024)}, u32[]{:S(2)}, u32[]{:S(2)}) %collective-permute-start.1) | collective-permute-done | bytes 884768 | tf_op jit(solution)/shard_map/ppermute | solution.py:13
  417.3 20.8 %collective-permute-done.2 = f32[221184]{0:T(1024)} collective-permute-done((f32[221184]{0:T(1024)}, f32[221184]{0:T(1024)}, u32[]{:S(2)}, u32[]{:S(2)}) %collective-permute-start.2) | collective-permute-done | bytes 884768 | tf_op jit(solution)/shard_map/ppermute | solution.py:13
  440.3 19.6 %collective-permute-done.3 = f32[221184]{0:T(1024)} collective-permute-done((f32[221184]{0:T(1024)}, f32[221184]{0:T(1024)}, u32[]{:S(2)}, u32[]{:S(2)}) %collective-permute-start.3) | collective-permute-done | bytes 884768 | tf_op jit(solution)/shard_map/ppermute | solution.py:13
  464.0 18.3 %collective-permute-done.4 = f32[221184]{0:T(1024)} collective-permute-done((f32[221184]{0:T(1024)}, f32[221184]{0:T(1024)}, u32[]{:S(2)}, u32[]{:S(2)}) %collective-permute-start.4) | collective-permute-done | bytes 884768 | tf_op jit(solution)/shard_map/ppermute | solution.py:13
  499.4 7.8 %scatter_fusion.1 = f32[128,64,128]{2,1,0:T(8,128)} fusion(f32[128,64,128]{2,1,0:T(8,128)} %broadcast.320, s32[44]{0:T(128)S(1)} %broadcast_subtract_fusion.1, f32[44,64,128]{2,1,0:T(8,128)} %bitcast.227), kind=kCustom, calls=%fused_computation.11 | custom fusion | flops 360448 | bytes 4325552 | tf_op jit(solution)/shard_map/scatter-add | solution.py:41
  507.5 10.1 %all_gather.45 = f32[8,64,128]{2,1,0:T(8,128)} all-gather(f32[2,64,128]{2,1,0:T(8,128)S(1)} %slice.243), channel_id=1, replica_groups=mesh['group'=4,'bulk'=32] {'group'}, dimensions={0}, use_global_device_ids=true | all-gather | bytes 327680 | tf_op jit(solution)/shard_map/all_gather | solution.py:34
  519.7 14.8 %all-gather.13.cloned.1.call-done = f32[128,64,128]{2,1,0:T(8,128)} async-done(((f32[4,64,128]{2,1,0:T(8,128)}), f32[128,64,128]{2,1,0:T(8,128)}) %all-gather.13.cloned.1.call-update) | async-done | bytes 4194320 | tf_op jit(solution)/shard_map/all_gather | solution.py:40
  538.5 5.4 fusion.15
  543.9 73.9 %reduce-scatter.5.cloned.1.call-done = f32[4,64,128]{2,1,0:T(8,128)} async-done(((f32[128,64,128]{2,1,0:T(8,128)}), f32[4,64,128]{2,1,0:T(8,128)}) %reduce-scatter.5.cloned.1.call-update) | async-done | bytes 131088 | tf_op jit(solution)/shard_map/reduce_scatter | solution.py:42
  622.1 68.0 %all-gather.21.cloned.1.call-done = f32[8192,64]{1,0:T(8,128)} async-done(((f32[64,64]{1,0:T(8,128)}), f32[8192,64]{1,0:T(8,128)}) %all-gather.21.cloned.1.call-update) | async-done | bytes 2097168 | tf_op jit(solution)/shard_map/all_gather | solution.py:24
  692.8 5.8 cholesky.81
  700.0 4.9 custom-call.17
  (170 shorter events, 130.2 us)
Async XLA Ops:
  7.2 137.9 %copy-start = (f32[2,4,128,128]{3,2,1,0:T(8,128)S(1)}, f32[2,4,128,128]{3,2,1,0:T(8,128)}, u32[]{:S(2)}) copy-start(f32[2,4,128,128]{3,2,1,0:T(8,128)} %param.29) | copy-start | bytes 1572868
  7.2 18.1 %copy-start.3 = (f32[4,64,128]{2,1,0:T(8,128)S(1)}, f32[4,64,128]{2,1,0:T(8,128)}, u32[]{:S(2)}) copy-start(f32[4,64,128]{2,1,0:T(8,128)} %param.26) | copy-start | bytes 393220
  7.2 16.2 %copy-start.2 = (s32[512]{0:T(512)S(1)}, s32[512]{0:T(512)}, u32[]{:S(2)}) copy-start(s32[512]{0:T(512)} %param.31) | copy-start | bytes 6148
  7.2 52.9 %all-gather.11.cloned.1.call-start = ((), (), s32[]{:S(2)}) async-start(), calls=%async_computation.2 | async-start | bytes 4325376 | tf_op jit(solution)/shard_map/all_gather | solution.py:40
  9.9 133.5 %reduce-scatter.3.cloned.1.call-start = ((), (), s32[]{:S(2)}) async-start(), calls=%async_computation.3 | async-start | bytes 4325376 | tf_op jit(solution)/shard_map/reduce_scatter | solution.py:42
  14.7 16.1 %copy-start.18 = (s32[1024]{0:T(1024)}, s32[1024]{0:T(1024)S(1)}, u32[]{:S(2)}) copy-start(s32[1024]{0:T(1024)S(1)} %pad_clamp_fusion.4) | copy-start | bytes 12292
  38.9 176.2 %all-gather.17.cloned.1.call-start = ((), (), s32[]{:S(2)}) async-start(), calls=%async_computation.7 | async-start | bytes 4227072 | tf_op jit(solution)/shard_map/all_gather | solution.py:24
  39.8 242.5 %all-gather.15.cloned.1.call-start = ((), (), s32[]{:S(2)}) async-start(), calls=%async_computation.6 | async-start | bytes 4227072 | tf_op jit(solution)/shard_map/all_gather | solution.py:24
  149.7 228.2 %all-gather.19.cloned.1.call-start = ((), (), s32[]{:S(2)}) async-start(), calls=%async_computation.8 | async-start | bytes 4227072 | tf_op jit(solution)/shard_map/all_gather | solution.py:24
  313.5 221.0 %all-gather.13.cloned.1.call-start = ((), (), s32[]{:S(2)}) async-start(), calls=%async_computation.4 | async-start | bytes 4325376 | tf_op jit(solution)/shard_map/all_gather | solution.py:40
  386.9 3.5 collective-permute-start
  392.6 21.3 %collective-permute-start.1 = (f32[221184]{0:T(1024)}, f32[221184]{0:T(1024)}, u32[]{:S(2)}, u32[]{:S(2)}) collective-permute-start(f32[221184]{0:T(1024)} %broadcast_select_fusion), channel_id=1, source_target_pairs={{0,2},{1,3},{2,0},{3,1},{4,6},{5,7},{6,4},{7,5},{8,10},{9,11},{10,... | collective-permute-start | bytes 2654216 | tf_op jit(solution)/shard_map/ppermute | solution.py:13
  416.1 47.1 %copy-start.21 = (s32[3]{0:T(128)S(1)}, s32[3]{0:T(128)}, u32[]{:S(2)}) copy-start(s32[3]{0:T(128)} %constant.238.clone.1) | copy-start | bytes 40
  416.1 47.9 %copy-start.11 = (f32[64,4,128]{2,0,1:T(8,128)S(1)}, f32[64,4,128]{2,0,1:T(8,128)}, u32[]{:S(2)}) copy-start(f32[64,4,128]{2,0,1:T(8,128)} %copy-done.10) | copy-start | bytes 393220
  416.1 22.0 %collective-permute-start.2 = (f32[221184]{0:T(1024)}, f32[221184]{0:T(1024)}, u32[]{:S(2)}, u32[]{:S(2)}) collective-permute-start(f32[221184]{0:T(1024)} %broadcast_select_fusion.1), channel_id=1, source_target_pairs={{0,4},{1,5},{2,6},{3,7},{4,0},{5,1},{6,2},{7,3},{8,12},{9,13},{10,... | collective-permute-start | bytes 2654216 | tf_op jit(solution)/shard_map/ppermute | solution.py:13
  440.3 19.6 %collective-permute-start.3 = (f32[221184]{0:T(1024)}, f32[221184]{0:T(1024)}, u32[]{:S(2)}, u32[]{:S(2)}) collective-permute-start(f32[221184]{0:T(1024)} %broadcast_select_fusion.2), channel_id=1, source_target_pairs={{0,8},{1,9},{2,10},{3,11},{4,12},{5,13},{6,14},{7,15},{8,0},{9,1},... | collective-permute-start | bytes 2654216 | tf_op jit(solution)/shard_map/ppermute | solution.py:13
  440.3 48.5 %copy-start.19 = (s32[4,11,1]{1,0,2:T(4,128)S(1)}, s32[4,11,1]{1,0,2:T(4,128)}, u32[]{:S(2)}) copy-start(s32[4,11,1]{1,0,2:T(4,128)} %get-tuple-element.96) | copy-start | bytes 532
  462.1 20.2 %collective-permute-start.4 = (f32[221184]{0:T(1024)}, f32[221184]{0:T(1024)}, u32[]{:S(2)}, u32[]{:S(2)}) collective-permute-start(f32[221184]{0:T(1024)} %broadcast_select_fusion.3), channel_id=1, source_target_pairs={{0,16},{1,17},{2,18},{3,19},{4,20},{5,21},{6,22},{7,23},{8,24},{9,... | collective-permute-start | bytes 2654216 | tf_op jit(solution)/shard_map/ppermute | solution.py:13
  487.2 130.6 %reduce-scatter.5.cloned.1.call-start = ((), (), s32[]{:S(2)}) async-start(), calls=%async_computation.5 | async-start | bytes 4325376 | tf_op jit(solution)/shard_map/reduce_scatter | solution.py:42
  507.2 182.9 %all-gather.21.cloned.1.call-start = ((), (), s32[]{:S(2)}) async-start(), calls=%async_computation.9 | async-start | bytes 4227072 | tf_op jit(solution)/shard_map/all_gather | solution.py:24
  619.5 85.5 %copy-start.12 = (f32[64,64]{1,0:T(8,128)S(1)}, f32[64,64]{1,0:T(8,128)}, u32[]{:S(2)}) copy-start(f32[64,64]{1,0:T(8,128)} %reduce_sum.38) | copy-start | bytes 49156
  619.5 85.5 %copy-start.16 = (f32[64,64]{0,1:T(8,128)S(1)}, f32[64,64]{0,1:T(8,128)}, u32[]{:S(2)}) copy-start(f32[64,64]{0,1:T(8,128)} %copy.48) | copy-start | bytes 49156
  619.5 85.9 %copy-start.7 = (f32[4,64,128]{2,1,0:T(8,128)S(1)}, f32[4,64,128]{2,1,0:T(8,128)}, u32[]{:S(2)}) copy-start(f32[4,64,128]{2,1,0:T(8,128)} %get-tuple-element.93) | copy-start | bytes 393220
  621.2 85.2 %copy-start.14 = (f32[4,64,128]{2,1,0:T(8,128)S(1)}, f32[4,64,128]{2,1,0:T(8,128)}, u32[]{:S(2)}) copy-start(f32[4,64,128]{2,1,0:T(8,128)} %copy-done.13) | copy-start | bytes 393220
  (11 other events, 17.5 us)
Sparse Core Ops, SparseCore 0:
  10.3 49.7 all-gather.10
  63.7 79.6 reduce-scatter.2
  147.2 67.8 all-gather.16
  218.1 64.1 all-gather.14
  313.6 64.2 all-gather.18
  487.4 47.0 all-gather.12
  538.1 79.6 reduce-scatter.4
  622.2 67.8 all-gather.20
